TPU v7x, 512 devices: a whole 4x8x8 slice. The times are simulated.
512 devices in a mesh: sec: 32 (over x, z), mpo: 16 (over y, core).
Axes of the slice: x: 4, y: 8, z: 8, core: 2. Of those that a mesh axis runs over, the one named last changes fastest.
Arguments:
- psi_blocks: bfloat16 [256, 256, 256], P('sec'), may hold values from -6 to 6
- left_env: bfloat16 [64, 256, 256], P('mpo'), may hold values from -0.375 to 0.375
- right_env: bfloat16 [64, 256, 256], P('mpo'), may hold values from -0.046875 to 0.046875
- dest_index: int32 [16, 32, 32, 1], P('mpo', 'sec'), may hold values from 0 to 31; in each aligned block of 32 rows (0 to 31, 32 to 63, ..., all dimensions but the last counted through in order) at most 2 rows name the same one
- dest_slot: int32 [16, 32, 32], P('mpo', 'sec'), may hold values from 0 to 7
Outputs:
- sigma_blocks: float32 [256, 256, 256], P('sec', 'mpo')
Inputs may be any that keep to these rules, and one draw needn't show every extreme that they name: `dest_index`: in the 32 pairs of one device (fixed j and i), at most 2 name the same index of sec, and some device has exactly 2 for one index.
All inputs are finite; a program needn't handle non-finite values.
Results may differ from a plain program's by a relative error of at most 0.0041.
Values may be sent and summed in bfloat16 or wider, within the bound.
No kernel may reach another device: no remote copies, remote signals or barrier semaphores. Data moves between devices by JAX's collectives and lax.ppermute only.
A program may use at most 128 MiB of HBM per device.

v0:
```python
import jax
import jax.numpy as jnp
from jax import lax
from jax.sharding import PartitionSpec as P


def on_device(psi_blocks, left_env, right_env, dest_index, dest_slot):
    sectors = psi_blocks.shape[0]
    width = psi_blocks.shape[1]
    shards = lax.axis_size("sec")
    lefts = lax.all_to_all(left_env, "mpo", split_axis=1, concat_axis=0, tiled=True)
    rights = lax.all_gather(right_env, "mpo", axis=0, tiled=True)
    target = dest_index[:, :, :, 0] * sectors + dest_slot
    targets = lax.all_gather(target[0], "mpo", axis=0, tiled=True).reshape(-1)
    half = jnp.einsum("wrb,sbc->wsrc", lefts, psi_blocks, preferred_element_type=jnp.float32)
    half = half.astype(jnp.bfloat16)
    full = jnp.einsum("wsrc,wcd->wsrd", half, rights, preferred_element_type=jnp.float32)
    full = full.astype(jnp.bfloat16)
    rows = full.shape[2]
    select = jnp.arange(shards * sectors, dtype=jnp.int32)[:, None] == targets[None, :]
    partial = jnp.dot(
        select.astype(jnp.bfloat16),
        full.reshape(-1, rows * width),
        preferred_element_type=jnp.float32,
    )
    partial = partial.reshape(shards * sectors, rows, width)
    return lax.psum_scatter(partial, "sec", scatter_dimension=0, tiled=True)


def solution(mesh):
    in_specs = (
        P("sec", None, None),
        P("mpo", None, None),
        P("mpo", None, None),
        P("mpo", "sec", None, None),
        P("mpo", "sec", None),
    )
    out_specs = P("sec", "mpo", None)
    return jax.shard_map(
        on_device, mesh=mesh, in_specs=in_specs, out_specs=out_specs, check_vma=False
    )
```

profile of v0, /device:TPU:16, one launch (start us, length us, event | category | flops | bytes accessed | tf_op | source)
XLA Modules:
  0.0 338.5 jit_solution(17519727256088023447)
XLA Ops:
  6.5 0.0 copy-start
  6.5 0.0 all-gather.3.cloned.1.call-start
  6.5 0.7 all-gather.3.cloned.1.call-update
  7.3 2.3 copy.13
  9.5 9.1 %all-to-all-start = ((bf16[4,256,256]{2,0,1:T(4,128)(2,1)}), bf16[4,256,256]{2,0,1:T(4,128)(2,1)S(1)}, u32[]{:S(2)}, u32[]{:S(2)}) async-start(bf16[4,256,256]{2,0,1:T(4,128)(2,1)} %copy.13), calls=%async_computation | async-start | bytes 1048576 | tf_op jit(solution)/shard_map/all_to_all | solution.py:11
  18.6 0.0 reduce-scatter.2.cloned.1.call-start
  18.7 0.7 bitcast_add_fusion
  19.4 24.9 %all-gather = s32[16,1,32]{2,1,0:T(1,128)S(1)} all-gather(s32[1,1,32]{2,1,0:T(1,128)S(1)} %bitcast_add_fusion), channel_id=2, replica_groups=mesh['sec'=32,'mpo'=16] {'mpo'}, dimensions={0}, use_global_device_ids=true | all-gather | bytes 2176 | tf_op jit(solution)/shard_map/all_gather | solution.py:14
  44.2 0.5 broadcast.13
  44.7 0.7 reduce.3
  45.4 0.1 eq.16
  45.5 0.0 all-to-all-done
  45.5 0.1 copy.14
  45.6 28.0 %all-gather.3.cloned.1.call-done = bf16[64,256,256]{2,1,0:T(8,128)(2,1)} async-done(((bf16[4,256,256]{2,1,0:T(8,128)(2,1)}), bf16[64,256,256]{2,1,0:T(8,128)(2,1)}) %all-gather.3.cloned.1.call-update) | async-done | bytes 8388624 | tf_op jit(solution)/shard_map/all_gather | solution.py:12
  73.6 0.0 copy-done
  73.6 7.7 %convert_bitcast_fusion = bf16[64,8,16,256]{3,2,1,0:T(8,128)(2,1)} fusion(bf16[64,256,256]{2,1,0:T(8,128)(2,1)} %all-gather.3.cloned.1.call-done, bf16[64,16,256,1]{2,1,3,0:T(8,128)(2,1)S(1)} %bitcast.40, bf16[8,256,256]{2,1,0:T(8,128)(2,1)S(1)} %copy-done), kind=kOutput, calls=%fused_computation.3 | convolution fusion | flops 2151677952 | bytes 14155776 | tf_op jit(solution)/shard_map/wsrc,wcd->wsrd/dot_general | solution.py:17
  81.3 6.3 %copy.20 = bf16[64,8,16,256]{3,1,2,0:T(8,128)(2,1)} copy(bf16[64,8,16,256]{3,2,1,0:T(8,128)(2,1)} %convert_bitcast_fusion) | data formatting | bytes 8388608
  87.7 6.5 %copy.16 = bf16[4096,512]{1,0:T(8,128)(2,1)} copy(bf16[4096,512]{0,1:T(8,128)(2,1)} %bitcast.39) | data formatting | bytes 8388608 | tf_op jit(solution)/shard_map/dot_general | solution.py:21
  94.2 5.4 %fusion.13 = f32[256,16,256]{2,0,1:T(8,128)} fusion(bf16[16,256,512]{2,1,0:T(8,128)(2,1)} %bitcast.38, s32[512]{0:T(512)S(1)} %eq.16), kind=kOutput, calls=%fused_computation.9 | convolution fusion | flops 1073872896 | bytes 8390656 | tf_op jit(solution)/shard_map/dot_general | solution.py:21
  99.6 0.0 reduce-scatter.2.cloned.1.call-update
  99.6 230.4 %reduce-scatter.2.cloned.1.call-done = f32[8,16,256]{2,0,1:T(8,128)} async-done(((f32[256,16,256]{2,0,1:T(8,128)}), f32[8,16,256]{2,0,1:T(8,128)}) %reduce-scatter.2.cloned.1.call-update) | async-done | bytes 131088 | tf_op jit(solution)/shard_map/reduce_scatter | solution.py:27
  330.1 1.6 copy.17
  (1 shorter events, 0.0 us)
Async XLA Ops:
  6.5 67.1 %copy-start = (bf16[8,256,256]{2,1,0:T(8,128)(2,1)S(1)}, bf16[8,256,256]{2,1,0:T(8,128)(2,1)}, u32[]{:S(2)}) copy-start(bf16[8,256,256]{2,1,0:T(8,128)(2,1)} %param.5) | copy-start | bytes 3145732
  6.5 67.1 %all-gather.3.cloned.1.call-start = ((), (), s32[]{:S(2)}) async-start(), calls=%async_computation.2 | async-start | bytes 8912896 | tf_op jit(solution)/shard_map/all_gather | solution.py:12
  9.5 35.9 %all-to-all-start = ((bf16[4,256,256]{2,0,1:T(4,128)(2,1)}), bf16[4,256,256]{2,0,1:T(4,128)(2,1)S(1)}, u32[]{:S(2)}, u32[]{:S(2)}) async-start(bf16[4,256,256]{2,0,1:T(4,128)(2,1)} %copy.13), calls=%async_computation | async-start | bytes 1048576 | tf_op jit(solution)/shard_map/all_to_all | solution.py:11
  18.6 311.4 %reduce-scatter.2.cloned.1.call-start = ((), (), s32[]{:S(2)}) async-start(), calls=%async_computation.3 | async-start | bytes 4325376 | tf_op jit(solution)/shard_map/reduce_scatter | solution.py:27
Sparse Core Ops, SparseCore 0:
  9.5 64.1 all-gather.2
  99.7 230.2 reduce-scatter.1
where the time goes:
time: 339 us
  waiting for transfers between devices  259 us (76%)
  blocking collectives  24.9 us (7%)
  local copies, waits for them, and re-layouts  17.4 us (5%)
  between operations  13.4 us (4%)
  matrix products  13.1 us (4%)
  starting transfers between devices  9.13 us (3%)
    reduce_scatter x1, waiting for transfers between devices, on_device(): return lax.psum_scatter(partial, 'sec', scatter_dimension=0, tiled=True)  230 us
    all_gather x1, waiting for transfers between devices, on_device(): rights = lax.all_gather(right_env, 'mpo', axis=0, tiled=True)  28 us
    all_gather x1, blocking collectives, on_device(): targets = lax.all_gather(target[0], 'mpo', axis=0, tiled=True).reshape(-1)  24.9 us
    all_to_all x1, starting transfers between devices, on_device(): lax.all_to_all(left_env, 'mpo', split_axis=1, concat_axis=0, tiled=True)  9.09 us
    unnamed x4, local copies, waits for them, and re-layouts  8.62 us
    dot_general x1, matrix products, on_device(): jnp.einsum('wsrc,wcd->wsrd', half, rights, preferred_element_type=jnp.flo...  7.7 us
  transfers between devices with their start and end apart: 3, of which 2 were waited for; matrix products, arithmetic and copies ran while one was open for 1% of the time, Pallas kernels for 0%

commit v1 on v0

--- a/solution.py
+++ b/solution.py
@@ -9,7 +9,9 @@
     width = psi_blocks.shape[1]
     shards = lax.axis_size("sec")
     lefts = lax.all_to_all(left_env, "mpo", split_axis=1, concat_axis=0, tiled=True)
-    rights = lax.all_gather(right_env, "mpo", axis=0, tiled=True)
+    rights = jnp.concatenate(
+        lax.all_to_all(jnp.stack([right_env] * lax.axis_size("mpo")), "mpo", 0, 0), axis=0
+    )
     target = dest_index[:, :, :, 0] * sectors + dest_slot
     targets = lax.all_gather(target[0], "mpo", axis=0, tiled=True).reshape(-1)
     half = jnp.einsum("wrb,sbc->wsrc", lefts, psi_blocks, preferred_element_type=jnp.float32)

time: 339 us -> 503 us (1.48)
  the two profiles are of different devices: /device:TPU:16 before, /device:TPU:8 now
where the time goes in v1:
time: 503 us
  waiting for transfers between devices  231 us (46%)
  blocking collectives  216 us (43%)
  local copies, waits for them, and re-layouts  22 us (4%)
  between operations  13.5 us (3%)
  matrix products  13.1 us (3%)
  starting transfers between devices  6.43 us (1%)
    reduce_scatter x1, waiting for transfers between devices, on_device(): return lax.psum_scatter(partial, 'sec', scatter_dimension=0, tiled=True)  231 us
    all_gather x1, blocking collectives, on_device(): targets = lax.all_gather(target[0], 'mpo', axis=0, tiled=True).reshape(-1)  193 us
    all_to_all x1, blocking collectives, on_device(): lax.all_to_all(left_env, 'mpo', split_axis=1, concat_axis=0, tiled=True)  22.6 us
  transfers between devices with their start and end apart: 2, of which 1 were waited for; matrix products, arithmetic and copies ran while one was open for 0% of the time, Pallas kernels for 0%

profile of v1, /device:TPU:8, one launch (start us, length us, event | category | flops | bytes accessed | tf_op | source)
XLA Modules:
  0.0 502.7 jit_solution(14457508075850010995)
XLA Ops:
  6.5 0.0 copy-start
  6.5 1.5 copy.13
  8.1 22.6 %all_to_all.23 = bf16[4,256,256]{2,0,1:T(4,128)(2,1)S(1)} all-to-all(bf16[4,256,256]{2,0,1:T(4,128)(2,1)S(1)} %copy.13), channel_id=1, replica_groups=mesh['sec'=32,'mpo'=16] {'mpo'}, dimensions={1} | all-to-all | bytes 1048576 | tf_op jit(solution)/shard_map/all_to_all | solution.py:11
  30.7 5.3 %stack.2 = bf16[16,4,256,256]{3,2,1,0:T(8,128)(2,1)} broadcast(bf16[4,256,256]{2,1,0:T(8,128)(2,1)} %param.7), dimensions={1,2,3} | broadcast | bytes 8912896 | tf_op jit(solution)/shard_map/stack | solution.py:13
  36.0 0.0 copy-start.1
  36.0 0.0 copy-start.2
  36.0 6.4 %all-to-all-start.1 = ((bf16[16,4,256,256]{3,2,1,0:T(8,128)(2,1)}), bf16[16,4,256,256]{3,2,1,0:T(8,128)(2,1)}, u32[]{:S(2)}, u32[]{:S(2)}) async-start(bf16[16,4,256,256]{3,2,1,0:T(8,128)(2,1)} %stack.2), calls=%async_computation.1 | async-start | bytes 16777216 | tf_op jit(solution)/shard_map/all_to_all | solution.py:13
  42.4 0.0 reduce-scatter.2.cloned.1.call-start
  42.4 0.0 copy-done.1
  42.4 0.0 copy-done.2
  42.5 192.9 %all-gather = s32[16,1,32]{2,1,0:T(1,128)S(1)} all-gather(s32[1,1,32]{2,1,0:T(1,128)S(1)} %bitcast_add_fusion), channel_id=2, replica_groups=mesh['sec'=32,'mpo'=16] {'mpo'}, dimensions={0}, use_global_device_ids=true | all-gather | bytes 2176 | tf_op jit(solution)/shard_map/all_gather | solution.py:16
  235.4 0.5 broadcast.15
  235.9 0.7 reduce.3
  236.6 0.1 eq.16
  236.7 0.1 copy.14
  236.8 0.0 all-to-all-done.1
  236.8 0.0 copy-done
  236.8 7.7 %convert_bitcast_fusion = bf16[64,8,16,256]{3,2,1,0:T(8,128)(2,1)} fusion(bf16[64,256,256,1]{2,1,3,0:T(8,128)(2,1)} %bitcast.11, bf16[64,16,256,1]{2,1,3,0:T(8,128)(2,1)S(1)} %bitcast.39, bf16[8,256,256]{2,1,0:T(8,128)(2,1)S(1)} %copy-done), kind=kOutput, calls=%fused_computation.2 | convolution fusion | flops 2151677952 | bytes 14155776 | tf_op jit(solution)/shard_map/wsrc,wcd->wsrd/dot_general | solution.py:19
  244.5 6.3 %copy.20 = bf16[64,8,16,256]{3,1,2,0:T(8,128)(2,1)} copy(bf16[64,8,16,256]{3,2,1,0:T(8,128)(2,1)} %convert_bitcast_fusion) | data formatting | bytes 8388608
  250.8 6.5 %copy.16 = bf16[4096,512]{1,0:T(8,128)(2,1)} copy(bf16[4096,512]{0,1:T(8,128)(2,1)} %bitcast.38) | data formatting | bytes 8388608 | tf_op jit(solution)/shard_map/dot_general | solution.py:23
  257.4 5.4 %fusion.10 = f32[256,16,256]{2,0,1:T(8,128)} fusion(bf16[16,256,512]{2,1,0:T(8,128)(2,1)} %bitcast.37, s32[512]{0:T(512)S(1)} %eq.16), kind=kOutput, calls=%fused_computation.8 | convolution fusion | flops 1073872896 | bytes 8390656 | tf_op jit(solution)/shard_map/dot_general | solution.py:23
  262.8 0.0 reduce-scatter.2.cloned.1.call-update
  262.8 231.5 %reduce-scatter.2.cloned.1.call-done = f32[8,16,256]{2,0,1:T(8,128)} async-done(((f32[256,16,256]{2,0,1:T(8,128)}), f32[8,16,256]{2,0,1:T(8,128)}) %reduce-scatter.2.cloned.1.call-update) | async-done | bytes 131088 | tf_op jit(solution)/shard_map/reduce_scatter | solution.py:29
  494.3 1.6 copy.17
  (2 shorter events, 0.0 us)
Async XLA Ops:
  6.5 230.3 %copy-start = (bf16[8,256,256]{2,1,0:T(8,128)(2,1)S(1)}, bf16[8,256,256]{2,1,0:T(8,128)(2,1)}, u32[]{:S(2)}) copy-start(bf16[8,256,256]{2,1,0:T(8,128)(2,1)} %param.5) | copy-start | bytes 3145732
  36.0 6.4 %copy-start.1 = (s32[1,1,32]{2,1,0:T(1,128)S(1)}, s32[1,1,32]{2,1,0:T(1,128)}, u32[]{:S(2)}) copy-start(s32[1,1,32]{2,1,0:T(1,128)} %param.9) | copy-start | bytes 388
  36.0 6.5 %copy-start.2 = (s32[1,1,32,1]{2,3,1,0:T(1,128)S(1)}, s32[1,1,32,1]{2,3,1,0:T(1,128)}, u32[]{:S(2)}) copy-start(s32[1,1,32,1]{2,3,1,0:T(1,128)} %param.8) | copy-start | bytes 388
  36.0 200.8 %all-to-all-start.1 = ((bf16[16,4,256,256]{3,2,1,0:T(8,128)(2,1)}), bf16[16,4,256,256]{3,2,1,0:T(8,128)(2,1)}, u32[]{:S(2)}, u32[]{:S(2)}) async-start(bf16[16,4,256,256]{3,2,1,0:T(8,128)(2,1)} %stack.2), calls=%async_computation.1 | async-start | bytes 16777216 | tf_op jit(solution)/shard_map/all_to_all | solution.py:13
  42.4 451.9 %reduce-scatter.2.cloned.1.call-start = ((), (), s32[]{:S(2)}) async-start(), calls=%async_computation.3 | async-start | bytes 4325376 | tf_op jit(solution)/shard_map/reduce_scatter | solution.py:29
Sparse Core Ops, SparseCore 0:
  262.9 231.3 reduce-scatter.1
